TPU v7x, 32 devices: a whole 2x2x4 slice. The times are simulated.
32 devices in a mesh: depth: 4 (over z), width: 2 (over x), hidden: 4 (over y, core).
Axes of the slice: x: 2, y: 2, z: 4, core: 2. Of those that a mesh axis runs over, the one named last changes fastest.
Arguments:
- inputs: float32 [4096, 3072], P('depth', 'width'), may hold values from -6 to 6
- weight: float32 [3072, 12288], P('width', ('hidden', 'depth')), may hold values from -0.15625 to 0.15625
- cotangent: float32 [4096, 12288], P('depth', 'hidden'), may hold values from -6 to 6
Outputs:
- input_grad: float32 [4096, 3072], P('depth', ('width', 'hidden'))
- weight_grad: float32 [3072, 12288], P('width', ('hidden', 'depth'))
All inputs are finite; a program needn't handle non-finite values.
Results may differ from a plain program's by a relative error of at most 0.00011.
Values sent between devices are 32-bit elements; how exact they have to be, the bound alone decides.
No kernel may reach another device: no remote copies, remote signals or barrier semaphores. Data moves between devices by JAX's collectives and lax.ppermute only.
A program may use at most 192 MiB of HBM per device.

v0:
```python
import jax
import jax.numpy as jnp
from jax import lax
from jax.sharding import PartitionSpec as P

inv_sqrt_two = 0.7071067811865476
inv_sqrt_two_pi = 0.3989422804014327


def gelu_slope(preact):
    cumulative = 0.5 * (1.0 + jax.scipy.special.erf(preact * inv_sqrt_two))
    density = jnp.exp(-0.5 * preact * preact) * inv_sqrt_two_pi
    return cumulative + preact * density


def product(left, right):
    return jnp.dot(left, right, precision=lax.Precision.HIGHEST, preferred_element_type=jnp.float32)


def product_last(left, right):
    return lax.dot_general(
        left,
        right,
        (((1,), (1,)), ((), ())),
        precision=lax.Precision.HIGHEST,
        preferred_element_type=jnp.float32,
    )


def product_first(left, right):
    return lax.dot_general(
        left,
        right,
        (((0,), (0,)), ((), ())),
        precision=lax.Precision.HIGHEST,
        preferred_element_type=jnp.float32,
    )


def local(inputs, weight, cotangent):
    full_weight = lax.all_gather(weight, "depth", axis=1, tiled=True)
    partial_value = product(inputs, full_weight)
    preact = lax.psum(partial_value, "width")
    pre_grad = cotangent * gelu_slope(preact)
    input_part = product_last(pre_grad, full_weight)
    input_grad = lax.psum_scatter(input_part, "hidden", scatter_dimension=1, tiled=True)
    weight_rows = lax.psum_scatter(
        product_first(pre_grad, inputs), "depth", scatter_dimension=0, tiled=True
    )
    return (input_grad, weight_rows.T)


def solution(mesh):
    placed = (P("depth", "width"), P("width", ("hidden", "depth")), P("depth", "hidden"))
    return jax.shard_map(
        local,
        mesh=mesh,
        in_specs=placed,
        out_specs=(P("depth", ("width", "hidden")), P("width", ("hidden", "depth"))),
        check_vma=False,
    )
```

profile of v0, /device:TPU:0, one launch (start us, length us, event | category | flops | bytes accessed | tf_op | source)
XLA Modules:
  0.0 1152.2 jit_solution(10877611028749341447)
XLA Ops:
  7.2 0.0 all-gather.2.cloned.1.call-start
  7.2 0.7 all-gather.2.cloned.1.call-update
  7.9 0.0 all-reduce.2.cloned.1.call-start
  7.9 326.9 %all-gather.2.cloned.1.call-done = f32[1536,3072]{1,0:T(8,128)} async-done(((f32[1536,768]{1,0:T(8,128)}), f32[1536,3072]{1,0:T(8,128)}) %all-gather.2.cloned.1.call-update) | async-done | bytes 18874384 | tf_op jit(solution)/shard_map/all_gather | solution.py:41
  334.9 68.7 %fusion.5 = f32[1024,3072]{1,0:T(8,128)} fusion(f32[1024,1536]{1,0:T(8,128)} %param.3, f32[1536,3072]{1,0:T(8,128)} %all-gather.2.cloned.1.call-done), kind=kOutput, calls=%fused_computation.6 | convolution fusion | flops 57982058496 | bytes 37748736 | tf_op jit(solution)/shard_map/dot_general | solution.py:17
  403.6 0.0 all-reduce.2.cloned.1.call-update
  403.6 0.0 reduce-scatter.5.cloned.1.call-start
  403.6 287.0 %all-reduce.2.cloned.1.call-done = f32[1024,3072]{1,0:T(8,128)} async-done(((f32[1024,3072]{1,0:T(8,128)}), f32[1024,3072]{1,0:T(8,128)}) %all-reduce.2.cloned.1.call-update) | async-done | bytes 12582928 | tf_op jit(solution)/shard_map/psum | solution.py:43
  690.6 10.8 fusion.4
  701.5 0.0 copy-start
  701.5 4.4 copy-done
  705.9 63.8 %fusion.7 = f32[3072,1536]{1,0:T(8,128)} fusion(f32[1024,3072]{1,0:T(8,128)S(1)} %fusion.4, f32[1024,1536]{1,0:T(8,128)} %param.3), kind=kOutput, calls=%fused_computation.8 | convolution fusion | flops 57982058496 | bytes 37748736 | tf_op jit(solution)/shard_map/dot_general | solution.py:31
  769.7 0.0 reduce-scatter.5.cloned.1.call-update
  769.7 0.0 reduce-scatter.3.cloned.1.call-start
  769.8 66.1 %fusion.6 = f32[1024,1536]{1,0:T(8,128)} fusion(f32[1024,3072]{1,0:T(8,128)} %copy-done, f32[1536,3072]{1,0:T(8,128)} %all-gather.2.cloned.1.call-done), kind=kOutput, calls=%fused_computation.7 | convolution fusion | flops 57982058496 | bytes 37748736 | tf_op jit(solution)/shard_map/dot_general | solution.py:21
  835.9 0.0 reduce-scatter.3.cloned.1.call-update
  835.9 247.9 %reduce-scatter.5.cloned.1.call-done = f32[768,1536]{1,0:T(8,128)} async-done(((f32[3072,1536]{1,0:T(8,128)}), f32[768,1536]{1,0:T(8,128)}) %reduce-scatter.5.cloned.1.call-update) | async-done | bytes 4718608 | tf_op jit(solution)/shard_map/reduce_scatter | solution.py:47
  1083.8 6.0 copy.5
  1089.9 55.8 %reduce-scatter.3.cloned.1.call-done = f32[1024,384]{1,0:T(8,128)} async-done(((f32[1024,1536]{1,0:T(8,128)}), f32[1024,384]{1,0:T(8,128)}) %reduce-scatter.3.cloned.1.call-update) | async-done | bytes 1572880 | tf_op jit(solution)/shard_map/reduce_scatter | solution.py:46
Async XLA Ops:
  7.2 327.7 %all-gather.2.cloned.1.call-start = ((), (), s32[]{:S(2)}) async-start(), calls=%async_computation.2 | async-start | bytes 23592960 | tf_op jit(solution)/shard_map/all_gather | solution.py:41
  7.9 682.8 %all-reduce.2.cloned.1.call-start = ((), (), s32[]{:S(2)}) async-start(), calls=%async_computation.3 | async-start | bytes 25165824 | tf_op jit(solution)/shard_map/psum | solution.py:43
  403.6 680.2 %reduce-scatter.5.cloned.1.call-start = ((), (), s32[]{:S(2)}) async-start(), calls=%async_computation.5 | async-start | bytes 23592960 | tf_op jit(solution)/shard_map/reduce_scatter | solution.py:47
  701.5 4.5 copy-start
  769.7 375.9 %reduce-scatter.3.cloned.1.call-start = ((), (), s32[]{:S(2)}) async-start(), calls=%async_computation.4 | async-start | bytes 7864320 | tf_op jit(solution)/shard_map/reduce_scatter | solution.py:46
Sparse Core Ops, SparseCore 0:
  9.6 325.2 all-gather.1
  403.7 286.8 all-reduce.1
  769.9 313.9 reduce-scatter.4
  1086.8 58.8 reduce-scatter.2
where the time goes:
time: 1150 us
  waiting for transfers between devices  918 us (80%)
  matrix products  199 us (17%)
  between operations  13.8 us (1%)
    all_gather x1, waiting for transfers between devices, local(): full_weight = lax.all_gather(weight, 'depth', axis=1, tiled=True)  327 us
    psum x1, waiting for transfers between devices, local(): preact = lax.psum(partial_value, 'width')  287 us
    reduce_scatter x1, waiting for transfers between devices, local(): lax.psum_scatter(product_first(pre_grad, inputs), 'depth', scatter_dimens...  248 us
    dot_general x1, matrix products, product(): jnp.dot(left, right, precision=lax.Precision.HIGHEST, preferred_element_t...  68.7 us
    dot_general x1, matrix products, product_last(): lax.dot_general(left, right, (((1,), (1,)), ((), ())), precision=lax.Prec...  66.1 us
    dot_general x1, matrix products, product_first(): lax.dot_general(left, right, (((0,), (0,)), ((), ())), precision=lax.Prec...  63.8 us
    reduce_scatter x1, waiting for transfers between devices, local(): lax.psum_scatter(input_part, 'hidden', scatter_dimension=1, tiled=True)  55.8 us
  transfers between devices with their start and end apart: 4, of which 4 were waited for; matrix products, arithmetic and copies ran while one was open for 6% of the time, Pallas kernels for 0%

commit v1 on v0

v1 whole, which is shorter than its diff:
```python
import jax
import jax.numpy as jnp
from jax import lax
from jax.sharding import PartitionSpec as P


inv_sqrt_two = 0.7071067811865476
inv_sqrt_two_pi = 0.3989422804014327

PARTS = (4, 7, 5)


def gelu_slope(preact):
    cumulative = 0.5 * (1.0 + jax.scipy.special.erf(preact * inv_sqrt_two))
    density = jnp.exp(-0.5 * preact * preact) * inv_sqrt_two_pi
    return cumulative + preact * density


def product(left, right, dims):
    return lax.dot_general(
        left,
        right,
        (dims, ((), ())),
        precision=lax.Precision.HIGH,
        preferred_element_type=jnp.float32,
    )


def make_local(mesh):
    depth, width, hidden = (mesh.shape[name] for name in ("depth", "width", "hidden"))
    pairs = hidden // 2

    def width_shift(values, by):
        return lax.ppermute(values, "width", [(i, (i + by) % width) for i in range(width)])

    def depth_shift(values, by):
        return lax.ppermute(values, "depth", [(i, (i + by) % depth) for i in range(depth)])

    def twin_swap(values):
        return lax.ppermute(values, "hidden", [(i, i ^ 1) for i in range(hidden)])

    def pair_shift(values, by):
        return lax.ppermute(
            values, "hidden", [(i, ((i // 2 + by) % pairs) * 2 + i % 2) for i in range(hidden)]
        )

    def up(values, first, last):
        return lax.ppermute(values, "depth", [(i, i + 1) for i in range(first, last)])

    def down(values, first, last):
        return lax.ppermute(
            values, "depth", [(depth - 1 - i, depth - 2 - i) for i in range(first, last)]
        )

    def local(inputs, weight, cotangent):
        tokens, model = inputs.shape
        units = weight.shape[1]
        block = model // hidden
        half = tokens // width
        sizes = [half * part // sum(PARTS) for part in PARTS]
        starts = [sum(sizes[:p]) for p in range(len(sizes))]
        z = lax.axis_index("depth")
        x = lax.axis_index("width")
        h = lax.axis_index("hidden")
        y, c = h // 2, h % 2
        order = [
            ((y + k) % pairs) * 2 + core
            for core in (1 - c, c)
            for k in [*range(1, pairs), 0]
        ]
        sides = [(x + k) % width for k in [*range(1, width), 0]]
        twin_weight, near_weight = (
            jnp.concatenate([lax.dynamic_slice_in_dim(weight, b * block, block, 0) for b in part])
            for part in (order[:pairs], order[pairs:])
        )

        def after(values, *others):
            return lax.optimization_barrier((values, *others))[0]

        gathered = []
        per_side = hidden // width
        for p, rows in enumerate(sizes):
            share = rows // per_side
            first = (h // per_side) * half + starts[p] + (h % per_side) * share
            piece = lax.dynamic_slice_in_dim(inputs, first, share, 0)
            below, above = [piece], [piece]
            for s in range(1, depth):
                below.append(up(below[-1], s - 1, depth - 1))
                above.append(down(above[-1], s - 1, depth - 1))
            column = jnp.stack(
                [jnp.where(z >= k, below[k], above[depth - k]) for k in range(1, depth)]
            )
            gathered.append(
                lax.all_gather(column, "hidden", axis=0, tiled=False)
            )

        def cot_rows(first, extent, column):
            return lax.dynamic_slice(cotangent, (first, column * units), (extent, units))

        def far_rows(p):
            parts = []
            for k in range(1, depth):
                piece = cot_rows(x * half + starts[p], sizes[p], (z + k) % depth)
                parts.append(depth_shift(piece, k))
            return parts

        def partials(blocks):
            sent = [product(b, weight, ((1,), (0,))) for b in blocks[:-1]]
            moved = [width_shift(s, k + 1) for k, s in enumerate(sent)]
            kept = product(blocks[-1], weight, ((1,), (0,)))
            return [after(kept, *sent), *moved]

        def slope_of(partial, cot):
            preact = partial[0]
            for part in partial[1:]:
                preact = preact + part
            return cot * gelu_slope(preact)

        def over_hidden(grad):
            twin_part = product(grad, twin_weight, ((1,), (1,)))
            twin_part = twin_swap(twin_part)
            near = product(grad, near_weight, ((1,), (1,))) + twin_part
            total = near[:, (pairs - 1) * block :]
            for k in range(1, pairs):
                moved = pair_shift(near[:, (k - 1) * block : k * block], k)
                total = total + moved
            return total

        def over_depth(sums):
            placed = jnp.concatenate(
                [
                    lax.dynamic_index_in_dim(sums, (z - d) % depth, 0, False).reshape(-1, block)
                    for d in range(depth)
                ]
            )
            placed = after(placed, *finished)
            total = lax.psum_scatter(placed, "depth", scatter_dimension=0, tiled=True)
            finished[:] = [total]
            return total

        weight_sum, gate, finished = [], [], []

        def weight_part(block_rows, grad):
            term = product(block_rows, grad, ((0,), (0,)))
            total = weight_sum[0] + term if weight_sum else term
            weight_sum[:] = [after(total)]

        def group(blocks, cot):
            partial = partials(blocks)
            grad = slope_of(partial, cot)
            others = [width_shift(grad, -k) for k in range(1, width)]
            gate[:] = [grad]
            own_sum = over_hidden(grad)
            weight_part(blocks[-1], grad)
            sums = []
            for k, g in enumerate(others):
                sums.append(over_hidden(g))
                weight_part(blocks[k], g)
            return [*sums, own_sum]

        blocks = [lax.dynamic_slice_in_dim(inputs, s * half, half, 0) for s in sides]
        totals = group(blocks, cot_rows(x * half, half, z))

        arrived = []
        for p, rows in enumerate(sizes):
            share = rows // per_side
            cots = far_rows(p)
            here = after(gathered[p], *gate)
            blocks = [
                lax.dynamic_slice_in_dim(here, s * per_side, per_side, 0).reshape(-1, model)
                for s in sides
            ]
            cot = jnp.stack([c.reshape(per_side, share, units) for c in cots], axis=1)
            sums = [
                [s.reshape(per_side, depth - 1, share, block)[:, k] for k in range(depth - 1)]
                for s in group(blocks, cot.reshape(-1, units))
            ]
            parts = []
            for q, side in enumerate(sums):
                base = totals[q][starts[p] : starts[p] + rows].reshape(per_side, share, block)
                parts.append(jnp.stack([base, *side]))
            if p < len(sizes) - 1:
                arrived.append(over_depth(jnp.stack(parts, axis=1)).reshape(width, rows, block))
            else:
                own = over_depth(parts[-1]).reshape(1, rows, block)
                others = over_depth(jnp.stack(parts[:-1], axis=1))
                arrived.append(jnp.concatenate([others.reshape(-1, rows, block), own]))
        stacked = jnp.concatenate(arrived, axis=1)
        input_grad = jnp.concatenate(
            [
                lax.dynamic_index_in_dim(stacked, (a - x - 1) % width, 0, keepdims=False)
                for a in range(width)
            ]
        )
        return input_grad, weight_sum[0]

    return local


def solution(mesh):
    placed = (P("depth", "width"), P("width", ("hidden", "depth")), P("depth", "hidden"))
    local = make_local(mesh)

    return jax.shard_map(
        local,
        mesh=mesh,
        in_specs=placed,
        out_specs=(P("depth", ("width", "hidden")), P("width", ("hidden", "depth"))),
        check_vma=False,
    )
```

time: 1150 us -> 602 us (0.52); the launches traced: 1150 us -> 590 us
  waiting for transfers between devices: 918 us -> 253 us
  starting transfers between devices: 0.16 us -> 78 us
  local copies, waits for them, and re-layouts: 10.5 us -> 39.3 us
  matrix products: 199 us -> 171 us
  other arithmetic: 10.8 us -> 32.3 us
    all_gather x1 -> x3, waiting for transfers between devices: 327 us -> 0.04 us  [local(): gathered.append(lax.all_gather(column, 'hidden', axis=0, tiled=False))]
    reduce_scatter x2 -> x4, waiting for transfers between devices: 304 us -> 0.01 us  [over_depth(): total = lax.psum_scatter(placed, 'depth', scatter_dimension=0, tiled=True)]
    psum x1 -> x0, waiting for transfers between devices: 287 us -> none  [local(): preact = lax.psum(partial_value, 'width')]
    ppermute x0 -> x51, waiting for transfers between devices: none -> 253 us  [the longest x8 101 us: width_shift(): lax.ppermute(values, 'width', [(i, (i + by) % width) for i in range(width)])]
    ppermute x0 -> x51, starting transfers between devices: none -> 77.4 us  [the longest x9 36.4 us: depth_shift(): lax.ppermute(values, 'depth', [(i, (i + by) % depth) for i in range(depth)])]
    dynamic_slice x0 -> x11, local copies, waits for them, and re-layouts: none -> 27.5 us  [the longest x3 12.5 us: local(): lax.dynamic_slice_in_dim(here, s * per_side, per_side, 0).reshape(-1, model)]
    dot_general x3 -> x32, matrix products: 199 us -> 171 us  [product(): lax.dot_general(left, right, (dims, ((), ())), precision=lax.Precision.HI...]
  transfers between devices with their start and end apart: 4 -> 58, of which waited for: 4 -> 21; matrix products, arithmetic and copies ran while one was open for 6% -> 39% of each run, Pallas kernels for 0% -> 0%
where the time goes in v1:
time: 602 us; the launch traced here: 590 us
  waiting for transfers between devices  253 us (42%)
  matrix products  171 us (28%)
  starting transfers between devices  78 us (13%)
  local copies, waits for them, and re-layouts  39.3 us (7%)
  other arithmetic  32.3 us (5%)
  between operations  16 us (3%)
    dot_general x32, matrix products, product(): lax.dot_general(left, right, (dims, ((), ())), precision=lax.Precision.HI...  171 us
    ppermute x8, waiting for transfers between devices, width_shift(): lax.ppermute(values, 'width', [(i, (i + by) % width) for i in range(width)])  101 us
    ppermute x9, waiting for transfers between devices, down(): lax.ppermute(values, 'depth', [(depth - 1 - i, depth - 2 - i) for i in ra...  67.1 us
    ppermute x8, waiting for transfers between devices, pair_shift(): lax.ppermute(values, 'hidden', [(i, (i // 2 + by) % pairs * 2 + i % 2) fo...  64 us
    ppermute x9, starting transfers between devices, depth_shift(): lax.ppermute(values, 'depth', [(i, (i + by) % depth) for i in range(depth)])  36.4 us
    ppermute x9, waiting for transfers between devices, up(): lax.ppermute(values, 'depth', [(i, i + 1) for i in range(first, last)])  17.8 us
    ppermute x9, starting transfers between devices, up(): lax.ppermute(values, 'depth', [(i, i + 1) for i in range(first, last)])  12.8 us
    dynamic_slice x3, local copies, waits for them, and re-layouts, local(): lax.dynamic_slice_in_dim(here, s * per_side, per_side, 0).reshape(-1, model)  12.5 us
  transfers between devices with their start and end apart: 58, of which 21 were waited for; matrix products, arithmetic and copies ran while one was open for 39% of the time, Pallas kernels for 0%

profile of v1, /device:TPU:0, one launch (start us, length us, event | category | flops | bytes accessed | tf_op | source)
XLA Modules:
  0.0 590.4 jit_solution(18411361082640624317)
XLA Ops:
  14.6 7.0 %collective-permute-done.7 = f32[64,1536]{1,0:T(8,128)S(1)} collective-permute-done((f32[64,1536]{1,0:T(8,128)S(1)}, f32[64,1536]{1,0:T(8,128)S(1)}, u32[]{:S(2)}, u32[]{:S(2)}) %collective-permute-start.7) | collective-permute-done | bytes 393248 | tf_op jit(solution)/shard_map/ppermute | solution.py:48
  27.7 9.7 %collective-permute-done.9 = f32[64,1536]{1,0:T(8,128)S(1)} collective-permute-done((f32[64,1536]{1,0:T(8,128)S(1)}, f32[64,1536]{1,0:T(8,128)S(1)}, u32[]{:S(2)}, u32[]{:S(2)}) %collective-permute-start.9) | collective-permute-done | bytes 393248 | tf_op jit(solution)/shard_map/ppermute | solution.py:51
  38.9 9.5 %collective-permute-done.10 = f32[64,1536]{1,0:T(8,128)S(1)} collective-permute-done((f32[64,1536]{1,0:T(8,128)S(1)}, f32[64,1536]{1,0:T(8,128)S(1)}, u32[]{:S(2)}, u32[]{:S(2)}) %collective-permute-start.10) | collective-permute-done | bytes 393248 | tf_op jit(solution)/shard_map/ppermute | solution.py:51
  53.6 10.7 %collective-permute-done.24 = f32[112,1536]{1,0:T(8,128)S(1)} collective-permute-done((f32[112,1536]{1,0:T(8,128)S(1)}, f32[112,1536]{1,0:T(8,128)S(1)}, u32[]{:S(2)}, u32[]{:S(2)}) %collective-permute-start.24) | collective-permute-done | bytes 688160 | tf_op jit(solution)/shard_map/ppermute | solution.py:48
  70.5 13.5 %collective-permute-done.26 = f32[112,1536]{1,0:T(8,128)S(1)} collective-permute-done((f32[112,1536]{1,0:T(8,128)S(1)}, f32[112,1536]{1,0:T(8,128)S(1)}, u32[]{:S(2)}, u32[]{:S(2)}) %collective-permute-start.26) | collective-permute-done | bytes 688160 | tf_op jit(solution)/shard_map/ppermute | solution.py:51
  85.4 13.2 %collective-permute-done.27 = f32[112,1536]{1,0:T(8,128)S(1)} collective-permute-done((f32[112,1536]{1,0:T(8,128)S(1)}, f32[112,1536]{1,0:T(8,128)S(1)}, u32[]{:S(2)}, u32[]{:S(2)}) %collective-permute-start.27) | collective-permute-done | bytes 688160 | tf_op jit(solution)/shard_map/ppermute | solution.py:51
  104.1 9.7 %fusion.1 = f32[512,768]{1,0:T(8,128)} fusion(f32[1536,768]{1,0:T(8,128)} %param.4, f32[1024,1536]{1,0:T(8,128)} %param.3, s32[]{:T(128)S(6)} %select_n.283), kind=kOutput, calls=%fused_computation.14 | convolution fusion | flops 3623878656 | bytes 9437188 | tf_op jit(solution)/shard_map/dot_general | solution.py:20
  124.9 8.5 %fusion.5 = f32[512,768]{1,0:T(8,128)} fusion(f32[1536,768]{1,0:T(8,128)} %param.4, f32[1024,1536]{1,0:T(8,128)} %param.3, s32[]{:T(128)S(6)} %select_n.281), kind=kOutput, calls=%fused_computation.18 | convolution fusion | flops 3623878656 | bytes 9437188 | tf_op jit(solution)/shard_map/dot_general | solution.py:20
  150.4 11.4 %collective-permute-start.21 = (f32[224,768]{1,0:T(8,128)}, f32[224,768]{1,0:T(8,128)}, u32[]{:S(2)}, u32[]{:S(2)}) collective-permute-start(f32[224,768]{1,0:T(8,128)} %get-tuple-element.25), channel_id=1, source_target_pairs={{0,8},{8,16},{16,24},{24,0},{1,9},{9,17},{17,25},{25,1},{2,10},{10... | collective-permute-start | bytes 2064392 | tf_op jit(solution)/shard_map/ppermute | solution.py:37
  165.6 14.3 %collective-permute-done.42 = f32[80,1536]{1,0:T(8,128)S(1)} collective-permute-done((f32[80,1536]{1,0:T(8,128)S(1)}, f32[80,1536]{1,0:T(8,128)S(1)}, u32[]{:S(2)}, u32[]{:S(2)}) %collective-permute-start.42) | collective-permute-done | bytes 491552 | tf_op jit(solution)/shard_map/ppermute | solution.py:51
  201.7 9.2 %collective-permute-done.1 = f32[512,768]{1,0:T(8,128)} collective-permute-done((f32[512,768]{1,0:T(8,128)}, f32[512,768]{1,0:T(8,128)}, u32[]{:S(2)}, u32[]{:S(2)}) %collective-permute-start.1) | collective-permute-done | bytes 1572896 | tf_op jit(solution)/shard_map/ppermute | solution.py:34
  231.4 17.3 %fusion.53 = f32[672,768]{1,0:T(8,128)} fusion(f32[672,1536]{1,0:T(8,128)S(1)} %bitcast.230, f32[1536,768]{1,0:T(8,128)S(1)} %bitcast.223), kind=kOutput, calls=%fused_computation.163 | convolution fusion | flops 4756340736 | bytes 10911744 | tf_op jit(solution)/shard_map/dot_general | solution.py:20
  292.4 29.2 %collective-permute-done.30 = f32[672,768]{1,0:T(8,128)} collective-permute-done((f32[672,768]{1,0:T(8,128)}, f32[672,768]{1,0:T(8,128)}, u32[]{:S(2)}, u32[]{:S(2)}) %collective-permute-start.30) | collective-permute-done | bytes 2064416 | tf_op jit(solution)/shard_map/ppermute | solution.py:34
  339.6 7.0 %collective-permute-done.20 = f32[384,384]{1,0:T(8,128)S(1)} collective-permute-done((f32[384,384]{1,0:T(8,128)S(1)}, f32[384,384]{1,0:T(8,128)S(1)}, u32[]{:S(2)}, u32[]{:S(2)}) %collective-permute-start.20) | collective-permute-done | bytes 589856 | tf_op jit(solution)/shard_map/ppermute | solution.py:43
  346.6 24.9 %collective-permute-done.31 = f32[672,768]{1,0:T(8,128)S(1)} collective-permute-done((f32[672,768]{1,0:T(8,128)S(1)}, f32[672,768]{1,0:T(8,128)S(1)}, u32[]{:S(2)}, u32[]{:S(2)}) %collective-permute-start.31) | collective-permute-done | bytes 2064416 | tf_op jit(solution)/shard_map/ppermute | solution.py:34
  406.1 8.2 %collective-permute-done.35 = f32[672,384]{1,0:T(8,128)S(1)} collective-permute-done((f32[672,384]{1,0:T(8,128)S(1)}, f32[672,384]{1,0:T(8,128)S(1)}, u32[]{:S(2)}, u32[]{:S(2)}) %collective-permute-start.35) | collective-permute-done | bytes 1032224 | tf_op jit(solution)/shard_map/ppermute | solution.py:43
  414.6 20.6 %collective-permute-done.33 = f32[672,384]{1,0:T(8,128)S(1)} collective-permute-done((f32[672,384]{1,0:T(8,128)S(1)}, f32[672,384]{1,0:T(8,128)S(1)}, u32[]{:S(2)}, u32[]{:S(2)}) %collective-permute-start.33) | collective-permute-done | bytes 1032224 | tf_op jit(solution)/shard_map/ppermute | solution.py:43
  444.4 30.3 %collective-permute-done.46 = f32[480,768]{1,0:T(8,128)S(1)} collective-permute-done((f32[480,768]{1,0:T(8,128)S(1)}, f32[480,768]{1,0:T(8,128)S(1)}, u32[]{:S(2)}, u32[]{:S(2)}) %collective-permute-start.46) | collective-permute-done | bytes 1474592 | tf_op jit(solution)/shard_map/ppermute | solution.py:34
  485.3 14.3 %collective-permute-done.50 = f32[480,384]{1,0:T(8,128)} collective-permute-done((f32[480,384]{1,0:T(8,128)}, f32[480,384]{1,0:T(8,128)}, u32[]{:S(2)}, u32[]{:S(2)}) %collective-permute-start.50) | collective-permute-done | bytes 737312 | tf_op jit(solution)/shard_map/ppermute | solution.py:43
  501.0 13.8 %collective-permute-done.48 = f32[480,384]{1,0:T(8,128)S(1)} collective-permute-done((f32[480,384]{1,0:T(8,128)S(1)}, f32[480,384]{1,0:T(8,128)S(1)}, u32[]{:S(2)}, u32[]{:S(2)}) %collective-permute-start.48) | collective-permute-done | bytes 737312 | tf_op jit(solution)/shard_map/ppermute | solution.py:43
  523.2 7.6 %convolution_add_fusion.1 = f32[1536,768]{1,0:T(8,128)S(1)} fusion(f32[1536,768]{1,0:T(8,128)S(1)} %fusion.3, f32[512,768]{1,0:T(8,128)} %collective-permute-done.1, f32[1024,1536]{1,0:T(8,128)} %param.3, s32[]{:T(128)S(6)} %select_n.283), kind=kOutput, calls=%fused_computation.9 | convolution fusion | flops 3625058304 | bytes 14155780 | tf_op jit(solution)/shard_map/dot_general | solution.py:20
  538.4 7.3 %convolution_add_fusion.2 = f32[1536,768]{1,0:T(8,128)} fusion(f32[1536,768]{1,0:T(8,128)S(1)} %add.455, f32[384,1536]{1,0:T(8,128)S(1)} %bitcast.235, f32[384,768]{1,0:T(8,128)} %collective-permute-done.14), kind=kOutput, calls=%fused_computation.10 | convolution fusion | flops 2719088640 | bytes 12976128 | tf_op jit(solution)/shard_map/dot_general | solution.py:20
  547.6 9.2 %fusion.57 = f32[1536,768]{1,0:T(8,128)S(1)} fusion(f32[672,1536]{1,0:T(8,128)} %bitcast.240, f32[672,768]{1,0:T(8,128)S(1)} %copy-done.20), kind=kOutput, calls=%fused_computation.167 | convolution fusion | flops 4756340736 | bytes 10911744 | tf_op jit(solution)/shard_map/dot_general | solution.py:20
  564.0 8.0 %convolution_add_fusion.3 = f32[1536,768]{1,0:T(8,128)S(1)} fusion(f32[1536,768]{1,0:T(8,128)S(1)} %add.457, f32[672,1536]{1,0:T(8,128)S(1)} %bitcast.231, f32[672,768]{1,0:T(8,128)S(1)} %copy-done.23), kind=kOutput, calls=%fused_computation.11 | convolution fusion | flops 4757520384 | bytes 15630336 | tf_op jit(solution)/shard_map/dot_general | solution.py:20
  (310 shorter events, 259.8 us)
Async XLA Ops:
  7.2 174.1 %all-gather.7.cloned.1.call-start = ((), (), s32[]{:S(2)}) async-start(), calls=%async_computation.8 | async-start | bytes 5898240 | tf_op jit(solution)/shard_map/all_gather | solution.py:94
  49.5 175.4 %all-gather.9.cloned.1.call-start = ((), (), s32[]{:S(2)}) async-start(), calls=%async_computation.9 | async-start | bytes 10321920 | tf_op jit(solution)/shard_map/all_gather | solution.py:94
  100.2 278.3 %all-gather.11.cloned.1.call-start = ((), (), s32[]{:S(2)}) async-start(), calls=%async_computation.10 | async-start | bytes 7372800 | tf_op jit(solution)/shard_map/all_gather | solution.py:94
  113.8 36.6 %collective-permute-start = (f32[512,768]{1,0:T(8,128)}, f32[512,768]{1,0:T(8,128)}, u32[]{:S(2)}, u32[]{:S(2)}) collective-permute-start(f32[512,768]{1,0:T(8,128)} %fusion.1), channel_id=1, source_target_pairs={{0,4},{4,0},{1,5},{5,1},{2,6},{6,2},{3,7},{7,3},{8,12},{12,8},{9,1... | collective-permute-start | bytes 4718600 | tf_op jit(solution)/shard_map/ppermute | solution.py:34
  117.5 70.8 %collective-permute-start.4 = (f32[128,768]{1,0:T(8,128)}, f32[128,768]{1,0:T(8,128)}, u32[]{:S(2)}, u32[]{:S(2)}) collective-permute-start(f32[128,768]{1,0:T(8,128)} %get-tuple-element.22), channel_id=1, source_target_pairs={{0,8},{8,16},{16,24},{24,0},{1,9},{9,17},{17,25},{25,1},{2,10},{10... | collective-permute-start | bytes 1179656 | tf_op jit(solution)/shard_map/ppermute | solution.py:37
  120.2 72.0 %collective-permute-start.5 = (f32[128,768]{1,0:T(8,128)}, f32[128,768]{1,0:T(8,128)}, u32[]{:S(2)}, u32[]{:S(2)}) collective-permute-start(f32[128,768]{1,0:T(8,128)} %get-tuple-element.24), channel_id=1, source_target_pairs={{0,16},{8,24},{16,0},{24,8},{1,17},{9,25},{17,1},{25,9},{2,18},{10... | collective-permute-start | bytes 1179656 | tf_op jit(solution)/shard_map/ppermute | solution.py:37
  140.5 53.2 %collective-permute-start.6 = (f32[128,768]{1,0:T(8,128)}, f32[128,768]{1,0:T(8,128)}, u32[]{:S(2)}, u32[]{:S(2)}) collective-permute-start(f32[128,768]{1,0:T(8,128)} %get-tuple-element.23), channel_id=1, source_target_pairs={{0,24},{8,0},{16,8},{24,16},{1,25},{9,1},{17,9},{25,17},{2,26},{10... | collective-permute-start | bytes 1179656 | tf_op jit(solution)/shard_map/ppermute | solution.py:37
  150.4 98.3 %collective-permute-start.21 = (f32[224,768]{1,0:T(8,128)}, f32[224,768]{1,0:T(8,128)}, u32[]{:S(2)}, u32[]{:S(2)}) collective-permute-start(f32[224,768]{1,0:T(8,128)} %get-tuple-element.25), channel_id=1, source_target_pairs={{0,8},{8,16},{16,24},{24,0},{1,9},{9,17},{17,25},{25,1},{2,10},{10... | collective-permute-start | bytes 2064392 | tf_op jit(solution)/shard_map/ppermute | solution.py:37
  181.2 257.3 %reduce-scatter.5.cloned.1.call-start = ((), (), s32[]{:S(2)}) async-start(), calls=%async_computation.4 | async-start | bytes 1966080 | tf_op jit(solution)/shard_map/reduce_scatter | solution.py:137
  188.3 60.9 %collective-permute-start.22 = (f32[224,768]{1,0:T(8,128)}, f32[224,768]{1,0:T(8,128)}, u32[]{:S(2)}, u32[]{:S(2)}) collective-permute-start(f32[224,768]{1,0:T(8,128)} %get-tuple-element.27), channel_id=1, source_target_pairs={{0,16},{8,24},{16,0},{24,8},{1,17},{9,25},{17,1},{25,9},{2,18},{10... | collective-permute-start | bytes 2064392 | tf_op jit(solution)/shard_map/ppermute | solution.py:37
  192.2 60.8 %collective-permute-start.23 = (f32[224,768]{1,0:T(8,128)}, f32[224,768]{1,0:T(8,128)}, u32[]{:S(2)}, u32[]{:S(2)}) collective-permute-start(f32[224,768]{1,0:T(8,128)} %get-tuple-element.26), channel_id=1, source_target_pairs={{0,24},{8,0},{16,8},{24,16},{1,25},{9,1},{17,9},{25,17},{2,26},{10... | collective-permute-start | bytes 2064392 | tf_op jit(solution)/shard_map/ppermute | solution.py:37
  210.9 48.6 %collective-permute-start.17 = (f32[512,768]{1,0:T(8,128)}, f32[512,768]{1,0:T(8,128)}, u32[]{:S(2)}, u32[]{:S(2)}) collective-permute-start(f32[512,768]{1,0:T(8,128)} %fusion.44), channel_id=1, source_target_pairs={{0,1},{1,0},{2,3},{3,2},{4,5},{5,4},{6,7},{7,6},{8,9},{9,8},{10,11... | collective-permute-start | bytes 4718600 | tf_op jit(solution)/shard_map/ppermute | solution.py:40
  223.4 41.1 %collective-permute-start.2 = (f32[512,768]{1,0:T(8,128)}, f32[512,768]{1,0:T(8,128)}, u32[]{:S(2)}, u32[]{:S(2)}) collective-permute-start(f32[512,768]{1,0:T(8,128)} %fusion.46), channel_id=1, source_target_pairs={{0,1},{1,0},{2,3},{3,2},{4,5},{5,4},{6,7},{7,6},{8,9},{9,8},{10,11... | collective-permute-start | bytes 4718600 | tf_op jit(solution)/shard_map/ppermute | solution.py:40
  249.1 72.5 %collective-permute-start.30 = (f32[672,768]{1,0:T(8,128)}, f32[672,768]{1,0:T(8,128)}, u32[]{:S(2)}, u32[]{:S(2)}) collective-permute-start(f32[672,768]{1,0:T(8,128)} %fusion.53), channel_id=1, source_target_pairs={{0,4},{4,0},{1,5},{5,1},{2,6},{6,2},{3,7},{7,3},{8,12},{12,8},{9,1... | collective-permute-start | bytes 6193160 | tf_op jit(solution)/shard_map/ppermute | solution.py:34
  264.5 59.7 %collective-permute-start.38 = (f32[160,768]{1,0:T(8,128)S(1)}, f32[160,768]{1,0:T(8,128)S(1)}, u32[]{:S(2)}, u32[]{:S(2)}) collective-permute-start(f32[160,768]{1,0:T(8,128)S(1)} %get-tuple-element.29), channel_id=1, source_target_pairs={{0,24},{8,0},{16,8},{24,16},{1,25},{9,1},{17,9},{25,17},{2,26},{10... | collective-permute-start | bytes 1474568 | tf_op jit(solution)/shard_map/ppermute | solution.py:37
  277.9 48.1 %collective-permute-start.18 = (f32[512,384]{1,0:T(8,128)S(1)}, f32[512,384]{1,0:T(8,128)S(1)}, u32[]{:S(2)}, u32[]{:S(2)}) collective-permute-start(f32[512,384]{1,0:T(8,128)S(1)} %slice.169), channel_id=1, source_target_pairs={{0,2},{1,3},{2,0},{3,1},{4,6},{5,7},{6,4},{7,5},{8,10},{9,11},{10,... | collective-permute-start | bytes 2359304 | tf_op jit(solution)/shard_map/ppermute | solution.py:43
  282.4 44.5 %collective-permute-start.19 = (f32[384,768]{1,0:T(8,128)S(1)}, f32[384,768]{1,0:T(8,128)S(1)}, u32[]{:S(2)}, u32[]{:S(2)}) collective-permute-start(f32[384,768]{1,0:T(8,128)S(1)} %fusion.43), channel_id=1, source_target_pairs={{0,1},{1,0},{2,3},{3,2},{4,5},{5,4},{6,7},{7,6},{8,9},{9,8},{10,11... | collective-permute-start | bytes 3538952 | tf_op jit(solution)/shard_map/ppermute | solution.py:40
  324.2 47.4 %collective-permute-start.31 = (f32[672,768]{1,0:T(8,128)S(1)}, f32[672,768]{1,0:T(8,128)S(1)}, u32[]{:S(2)}, u32[]{:S(2)}) collective-permute-start(f32[672,768]{1,0:T(8,128)S(1)} %fusion.11), channel_id=1, source_target_pairs={{0,4},{4,0},{1,5},{5,1},{2,6},{6,2},{3,7},{7,3},{8,12},{12,8},{9,1... | collective-permute-start | bytes 6193160 | tf_op jit(solution)/shard_map/ppermute | solution.py:34
  334.9 40.8 %collective-permute-start.16 = (f32[384,384]{1,0:T(8,128)S(1)}, f32[384,384]{1,0:T(8,128)S(1)}, u32[]{:S(2)}, u32[]{:S(2)}) collective-permute-start(f32[384,384]{1,0:T(8,128)S(1)} %slice.164), channel_id=1, source_target_pairs={{0,2},{1,3},{2,0},{3,1},{4,6},{5,7},{6,4},{7,5},{8,10},{9,11},{10,... | collective-permute-start | bytes 1769480 | tf_op jit(solution)/shard_map/ppermute | solution.py:43
  339.6 42.3 %collective-permute-start.34 = (f32[672,768]{1,0:T(8,128)}, f32[672,768]{1,0:T(8,128)}, u32[]{:S(2)}, u32[]{:S(2)}) collective-permute-start(f32[672,768]{1,0:T(8,128)} %fusion.41), channel_id=1, source_target_pairs={{0,1},{1,0},{2,3},{3,2},{4,5},{5,4},{6,7},{7,6},{8,9},{9,8},{10,11... | collective-permute-start | bytes 6193160 | tf_op jit(solution)/shard_map/ppermute | solution.py:40
  378.3 138.0 %reduce-scatter.7.cloned.1.call-start = ((), (), s32[]{:S(2)}) async-start(), calls=%async_computation.5 | async-start | bytes 3440640 | tf_op jit(solution)/shard_map/reduce_scatter | solution.py:137
  395.3 43.3 %collective-permute-start.45 = (f32[480,768]{1,0:T(8,128)}, f32[480,768]{1,0:T(8,128)}, u32[]{:S(2)}, u32[]{:S(2)}) collective-permute-start(f32[480,768]{1,0:T(8,128)} %fusion.55), channel_id=1, source_target_pairs={{0,4},{4,0},{1,5},{5,1},{2,6},{6,2},{3,7},{7,3},{8,12},{12,8},{9,1... | collective-permute-start | bytes 4423688 | tf_op jit(solution)/shard_map/ppermute | solution.py:34
  438.5 108.1 %reduce-scatter.9.cloned.1.call-start = ((), (), s32[]{:S(2)}) async-start(), calls=%async_computation.6 | async-start | bytes 1228800 | tf_op jit(solution)/shard_map/reduce_scatter | solution.py:137
  516.3 64.4 %reduce-scatter.11.cloned.1.call-start = ((), (), s32[]{:S(2)}) async-start(), calls=%async_computation.7 | async-start | bytes 1228800 | tf_op jit(solution)/shard_map/reduce_scatter | solution.py:137
  (87 other events, 1091.7 us)
Sparse Core Ops, SparseCore 0:
  49.7 35.8 all-gather.6
  100.3 55.7 all-gather.8
  181.3 45.8 all-gather.10
  378.4 37.6 reduce-scatter.4
  438.6 56.4 reduce-scatter.6
  516.4 28.4 reduce-scatter.8
  547.8 27.1 reduce-scatter.10

commit v2 on v1

--- a/solution.py
+++ b/solution.py
@@ -176,16 +176,10 @@
                 for s in group(blocks, cot.reshape(-1, units))
             ]
             parts = []
-            for q, side in enumerate(sums):
-                base = totals[q][starts[p] : starts[p] + rows].reshape(per_side, share, block)
-                parts.append(jnp.stack([base, *side]))
-            if p < len(sizes) - 1:
-                arrived.append(over_depth(jnp.stack(parts, axis=1)).reshape(width, rows, block))
-            else:
-                own = over_depth(parts[-1]).reshape(1, rows, block)
-                others = over_depth(jnp.stack(parts[:-1], axis=1))
-                arrived.append(jnp.concatenate([others.reshape(-1, rows, block), own]))
-        stacked = jnp.concatenate(arrived, axis=1)
+            for side in sums:
+                parts.append(jnp.stack([jnp.zeros_like(side[0]), *side]))
+            arrived.append(over_depth(jnp.stack(parts, axis=1)).reshape(width, rows, block))
+        stacked = jnp.concatenate(arrived, axis=1) + jnp.stack(totals)
         input_grad = jnp.concatenate(
             [
                 lax.dynamic_index_in_dim(stacked, (a - x - 1) % width, 0, keepdims=False)

time: 602 us -> 635 us (1.055)
  the two profiles are of different devices: /device:TPU:0 before, /device:TPU:8 now
where the time goes in v2:
time: 635 us; the launch traced here: 626 us
  waiting for transfers between devices  278 us (44%)
  matrix products  176 us (28%)
  starting transfers between devices  78.3 us (12%)
  other arithmetic  39.2 us (6%)
  local copies, waits for them, and re-layouts  38.9 us (6%)
  between operations  15.4 us (2%)
    dot_general x32, matrix products, product(): lax.dot_general(left, right, (dims, ((), ())), precision=lax.Precision.HI...  176 us
    ppermute x9, waiting for transfers between devices, depth_shift(): lax.ppermute(values, 'depth', [(i, (i + by) % depth) for i in range(depth)])  105 us
    ppermute x8, waiting for transfers between devices, width_shift(): lax.ppermute(values, 'width', [(i, (i + by) % width) for i in range(width)])  56.5 us
    ppermute x8, waiting for transfers between devices, pair_shift(): lax.ppermute(values, 'hidden', [(i, (i // 2 + by) % pairs * 2 + i % 2) fo...  53.4 us
    ppermute x9, waiting for transfers between devices, up(): lax.ppermute(values, 'depth', [(i, i + 1) for i in range(first, last)])  35 us
    ppermute x9, waiting for transfers between devices, down(): lax.ppermute(values, 'depth', [(depth - 1 - i, depth - 2 - i) for i in ra...  28.1 us
    ppermute x9, starting transfers between devices, down(): lax.ppermute(values, 'depth', [(depth - 1 - i, depth - 2 - i) for i in ra...  27.6 us
    ppermute x9, starting transfers between devices, up(): lax.ppermute(values, 'depth', [(i, i + 1) for i in range(first, last)])  19.1 us
  transfers between devices with their start and end apart: 57, of which 28 were waited for; matrix products, arithmetic and copies ran while one was open for 39% of the time, Pallas kernels for 0%

profile of v2, /device:TPU:8, one launch (start us, length us, event | category | flops | bytes accessed | tf_op | source)
XLA Modules:
  0.0 625.6 jit_solution(6383993979719674969)
XLA Ops:
  14.1 6.9 %collective-permute-done.3 = f32[64,1536]{1,0:T(8,128)S(1)} collective-permute-done((f32[64,1536]{1,0:T(8,128)S(1)}, f32[64,1536]{1,0:T(8,128)S(1)}, u32[]{:S(2)}, u32[]{:S(2)}) %collective-permute-start.3) | collective-permute-done | bytes 393248 | tf_op jit(solution)/shard_map/ppermute | solution.py:48
  53.2 10.6 %collective-permute-done.19 = f32[112,1536]{1,0:T(8,128)S(1)} collective-permute-done((f32[112,1536]{1,0:T(8,128)S(1)}, f32[112,1536]{1,0:T(8,128)S(1)}, u32[]{:S(2)}, u32[]{:S(2)}) %collective-permute-start.19) | collective-permute-done | bytes 688160 | tf_op jit(solution)/shard_map/ppermute | solution.py:48
  69.4 8.0 %collective-permute-done.23 = f32[112,1536]{1,0:T(8,128)S(1)} collective-permute-done((f32[112,1536]{1,0:T(8,128)S(1)}, f32[112,1536]{1,0:T(8,128)S(1)}, u32[]{:S(2)}, u32[]{:S(2)}) %collective-permute-start.23) | collective-permute-done | bytes 688160 | tf_op jit(solution)/shard_map/ppermute | solution.py:48
  85.1 10.1 %collective-permute-done.22 = f32[112,1536]{1,0:T(8,128)S(1)} collective-permute-done((f32[112,1536]{1,0:T(8,128)S(1)}, f32[112,1536]{1,0:T(8,128)S(1)}, u32[]{:S(2)}, u32[]{:S(2)}) %collective-permute-start.22) | collective-permute-done | bytes 688160 | tf_op jit(solution)/shard_map/ppermute | solution.py:51
  117.2 7.4 %fusion.1 = f32[512,768]{1,0:T(8,128)S(1)} fusion(f32[1536,768]{1,0:T(8,128)} %param.4, f32[1024,1536]{1,0:T(8,128)} %param.3, s32[]{:T(128)S(6)} %select_n.285), kind=kOutput, calls=%fused_computation.22 | convolution fusion | flops 3623878656 | bytes 9437188 | tf_op jit(solution)/shard_map/dot_general | solution.py:20
  126.2 7.4 %fusion.5 = f32[512,768]{1,0:T(8,128)S(1)} fusion(f32[1536,768]{1,0:T(8,128)} %param.4, f32[1024,1536]{1,0:T(8,128)} %param.3, s32[]{:T(128)S(6)} %select_n.283), kind=kOutput, calls=%fused_computation.26 | convolution fusion | flops 3623878656 | bytes 9437188 | tf_op jit(solution)/shard_map/dot_general | solution.py:20
  144.9 7.8 %collective-permute-done.9 = f32[512,768]{1,0:T(8,128)} collective-permute-done((f32[512,768]{1,0:T(8,128)S(1)}, f32[512,768]{1,0:T(8,128)}, u32[]{:S(2)}, u32[]{:S(2)}) %collective-permute-start.9) | collective-permute-done | bytes 1572896 | tf_op jit(solution)/shard_map/ppermute | solution.py:34
  171.5 18.7 %collective-permute-done = f32[128,768]{1,0:T(8,128)} collective-permute-done((f32[128,768]{1,0:T(8,128)}, f32[128,768]{1,0:T(8,128)}, u32[]{:S(2)}, u32[]{:S(2)}) %collective-permute-start) | collective-permute-done | bytes 393248 | tf_op jit(solution)/shard_map/ppermute | solution.py:37
  211.9 6.6 %fusion.59 = f32[672,768]{1,0:T(8,128)} fusion(f32[672,1536]{1,0:T(8,128)S(1)} %bitcast.226, f32[1536,768]{1,0:T(8,128)S(1)} %bitcast.217), kind=kOutput, calls=%fused_computation.168 | convolution fusion | flops 4756340736 | bytes 10911744 | tf_op jit(solution)/shard_map/dot_general | solution.py:20
  229.7 38.7 %collective-permute-done.16 = f32[224,768]{1,0:T(8,128)} collective-permute-done((f32[224,768]{1,0:T(8,128)}, f32[224,768]{1,0:T(8,128)}, u32[]{:S(2)}, u32[]{:S(2)}) %collective-permute-start.16) | collective-permute-done | bytes 688160 | tf_op jit(solution)/shard_map/ppermute | solution.py:37
  268.5 11.2 %collective-permute-done.17 = f32[224,768]{1,0:T(8,128)} collective-permute-done((f32[224,768]{1,0:T(8,128)}, f32[224,768]{1,0:T(8,128)}, u32[]{:S(2)}, u32[]{:S(2)}) %collective-permute-start.17) | collective-permute-done | bytes 688160 | tf_op jit(solution)/shard_map/ppermute | solution.py:37
  319.6 25.9 %collective-permute-done.32 = f32[160,768]{1,0:T(8,128)} collective-permute-done((f32[160,768]{1,0:T(8,128)}, f32[160,768]{1,0:T(8,128)}, u32[]{:S(2)}, u32[]{:S(2)}) %collective-permute-start.32) | collective-permute-done | bytes 491552 | tf_op jit(solution)/shard_map/ppermute | solution.py:37
  394.9 15.6 %collective-permute-done.40 = f32[480,768]{1,0:T(8,128)} collective-permute-done((f32[480,768]{1,0:T(8,128)}, f32[480,768]{1,0:T(8,128)}, u32[]{:S(2)}, u32[]{:S(2)}) %collective-permute-start.40) | collective-permute-done | bytes 1474592 | tf_op jit(solution)/shard_map/ppermute | solution.py:34
  415.0 15.4 %collective-permute-done.28 = f32[672,384]{1,0:T(8,128)S(1)} collective-permute-done((f32[672,384]{1,0:T(8,128)S(1)}, f32[672,384]{1,0:T(8,128)S(1)}, u32[]{:S(2)}, u32[]{:S(2)}) %collective-permute-start.28) | collective-permute-done | bytes 1032224 | tf_op jit(solution)/shard_map/ppermute | solution.py:43
  439.6 9.7 %collective-permute-done.41 = f32[480,768]{1,0:T(8,128)} collective-permute-done((f32[480,768]{1,0:T(8,128)}, f32[480,768]{1,0:T(8,128)}, u32[]{:S(2)}, u32[]{:S(2)}) %collective-permute-start.41) | collective-permute-done | bytes 1474592 | tf_op jit(solution)/shard_map/ppermute | solution.py:34
  457.7 23.4 %collective-permute-done.46 = f32[512,768]{1,0:T(8,128)S(1)} collective-permute-done((f32[512,768]{1,0:T(8,128)}, f32[512,768]{1,0:T(8,128)S(1)}, u32[]{:S(2)}, u32[]{:S(2)}) %collective-permute-start.46) | collective-permute-done | bytes 1572896 | tf_op jit(solution)/shard_map/ppermute | solution.py:34
  484.5 9.1 %fusion.3 = f32[1536,768]{1,0:T(8,128)} fusion(f32[512,768]{1,0:T(8,128)} %fusion.16, f32[1024,1536]{1,0:T(8,128)} %param.3, s32[]{:T(128)S(6)} %select_n.283), kind=kOutput, calls=%fused_computation.24 | convolution fusion | flops 3623878656 | bytes 9437188 | tf_op jit(solution)/shard_map/dot_general | solution.py:20
  517.0 15.7 %collective-permute-done.43 = f32[480,384]{1,0:T(8,128)S(1)} collective-permute-done((f32[480,384]{1,0:T(8,128)S(1)}, f32[480,384]{1,0:T(8,128)S(1)}, u32[]{:S(2)}, u32[]{:S(2)}) %collective-permute-start.43) | collective-permute-done | bytes 737312 | tf_op jit(solution)/shard_map/ppermute | solution.py:43
  536.2 8.6 %convolution_add_fusion.1 = f32[1536,768]{1,0:T(8,128)S(1)} fusion(f32[1536,768]{1,0:T(8,128)} %fusion.3, f32[512,768]{1,0:T(8,128)S(1)} %copy-done.22, f32[1024,1536]{1,0:T(8,128)} %param.3, s32[]{:T(128)S(6)} %select_n.285), kind=kOutput, calls=%fused_computation.9 | convolution fusion | flops 3625058304 | bytes 14155780 | tf_op jit(solution)/shard_map/dot_general | solution.py:20
  550.9 15.0 %collective-permute-done.48 = f32[512,384]{1,0:T(8,128)S(1)} collective-permute-done((f32[512,384]{1,0:T(8,128)S(1)}, f32[512,384]{1,0:T(8,128)S(1)}, u32[]{:S(2)}, u32[]{:S(2)}) %collective-permute-start.48) | collective-permute-done | bytes 786464 | tf_op jit(solution)/shard_map/ppermute | solution.py:43
  579.8 8.8 %fusion.63 = f32[1536,768]{1,0:T(8,128)S(1)} fusion(f32[672,1536]{1,0:T(8,128)S(1)} %bitcast.235, f32[672,768]{1,0:T(8,128)} %fusion.11), kind=kOutput, calls=%fused_computation.172 | convolution fusion | flops 4756340736 | bytes 10911744 | tf_op jit(solution)/shard_map/dot_general | solution.py:20
  590.5 6.6 %fusion.64 = f32[1536,768]{1,0:T(8,128)S(1)} fusion(f32[480,1536]{1,0:T(8,128)S(1)} %bitcast.225, f32[480,768]{1,0:T(8,128)} %fusion.21), kind=kOutput, calls=%fused_computation.173 | convolution fusion | flops 3397386240 | bytes 9142272 | tf_op jit(solution)/shard_map/dot_general | solution.py:20
  597.1 9.2 %convolution_add_fusion.3 = f32[1536,768]{1,0:T(8,128)S(1)} fusion(f32[1536,768]{1,0:T(8,128)S(1)} %add.450, f32[672,1536]{1,0:T(8,128)S(1)} %bitcast.227, f32[672,768]{1,0:T(8,128)} %collective-permute-done.26), kind=kOutput, calls=%fused_computation.11 | convolution fusion | flops 4757520384 | bytes 15630336 | tf_op jit(solution)/shard_map/dot_general | solution.py:20
  608.2 7.8 %convolution_add_fusion = f32[1536,768]{1,0:T(8,128)} fusion(f32[1536,768]{1,0:T(8,128)S(1)} %add.452, f32[480,1536]{1,0:T(8,128)S(1)} %bitcast.229, f32[480,768]{1,0:T(8,128)} %collective-permute-done.41), kind=kOutput, calls=%fused_computation.8 | convolution fusion | flops 3398565888 | bytes 13860864 | tf_op jit(solution)/shard_map/dot_general | solution.py:20
  (291 shorter events, 306.2 us)
Async XLA Ops:
  7.2 149.3 %all-gather.7.cloned.1.call-start = ((), (), s32[]{:S(2)}) async-start(), calls=%async_computation.6 | async-start | bytes 5898240 | tf_op jit(solution)/shard_map/all_gather | solution.py:94
  46.1 159.5 %all-gather.9.cloned.1.call-start = ((), (), s32[]{:S(2)}) async-start(), calls=%async_computation.7 | async-start | bytes 10321920 | tf_op jit(solution)/shard_map/all_gather | solution.py:94
  96.7 269.2 %all-gather.11.cloned.1.call-start = ((), (), s32[]{:S(2)}) async-start(), calls=%async_computation.8 | async-start | bytes 7372800 | tf_op jit(solution)/shard_map/all_gather | solution.py:94
  144.6 288.3 %reduce-scatter.4.cloned.1.call-start = ((), (), s32[]{:S(2)}) async-start(), calls=%async_computation.3 | async-start | bytes 1966080 | tf_op jit(solution)/shard_map/reduce_scatter | solution.py:137
  164.5 38.9 %collective-permute-start.10 = (f32[384,768]{1,0:T(8,128)}, f32[384,768]{1,0:T(8,128)S(1)}, u32[]{:S(2)}, u32[]{:S(2)}) collective-permute-start(f32[384,768]{1,0:T(8,128)} %fusion.57), channel_id=1, source_target_pairs={{0,4},{4,0},{1,5},{5,1},{2,6},{6,2},{3,7},{7,3},{8,12},{12,8},{9,1... | collective-permute-start | bytes 3538952 | tf_op jit(solution)/shard_map/ppermute | solution.py:34
  205.0 82.0 %collective-permute-start.11 = (f32[384,768]{1,0:T(8,128)}, f32[384,768]{1,0:T(8,128)}, u32[]{:S(2)}, u32[]{:S(2)}) collective-permute-start(f32[384,768]{1,0:T(8,128)} %fusion.26), channel_id=1, source_target_pairs={{0,4},{4,0},{1,5},{5,1},{2,6},{6,2},{3,7},{7,3},{8,12},{12,8},{9,1... | collective-permute-start | bytes 3538952 | tf_op jit(solution)/shard_map/ppermute | solution.py:34
  218.5 78.7 %collective-permute-start.25 = (f32[672,768]{1,0:T(8,128)}, f32[672,768]{1,0:T(8,128)}, u32[]{:S(2)}, u32[]{:S(2)}) collective-permute-start(f32[672,768]{1,0:T(8,128)} %fusion.59), channel_id=1, source_target_pairs={{0,4},{4,0},{1,5},{5,1},{2,6},{6,2},{3,7},{7,3},{8,12},{12,8},{9,1... | collective-permute-start | bytes 6193160 | tf_op jit(solution)/shard_map/ppermute | solution.py:34
  222.8 45.6 %collective-permute-start.16 = (f32[224,768]{1,0:T(8,128)}, f32[224,768]{1,0:T(8,128)}, u32[]{:S(2)}, u32[]{:S(2)}) collective-permute-start(f32[224,768]{1,0:T(8,128)} %get-tuple-element.23), channel_id=1, source_target_pairs={{0,8},{8,16},{16,24},{24,0},{1,9},{9,17},{17,25},{25,1},{2,10},{10... | collective-permute-start | bytes 2064392 | tf_op jit(solution)/shard_map/ppermute | solution.py:37
  222.8 56.8 %collective-permute-start.17 = (f32[224,768]{1,0:T(8,128)}, f32[224,768]{1,0:T(8,128)}, u32[]{:S(2)}, u32[]{:S(2)}) collective-permute-start(f32[224,768]{1,0:T(8,128)} %get-tuple-element.25), channel_id=1, source_target_pairs={{0,16},{8,24},{16,0},{24,8},{1,17},{9,25},{17,1},{25,9},{2,18},{10... | collective-permute-start | bytes 2064392 | tf_op jit(solution)/shard_map/ppermute | solution.py:37
  224.8 56.3 %collective-permute-start.18 = (f32[224,768]{1,0:T(8,128)}, f32[224,768]{1,0:T(8,128)}, u32[]{:S(2)}, u32[]{:S(2)}) collective-permute-start(f32[224,768]{1,0:T(8,128)} %get-tuple-element.24), channel_id=1, source_target_pairs={{0,24},{8,0},{16,8},{24,16},{1,25},{9,1},{17,9},{25,17},{2,26},{10... | collective-permute-start | bytes 2064392 | tf_op jit(solution)/shard_map/ppermute | solution.py:37
  300.4 58.0 %collective-permute-start.26 = (f32[672,768]{1,0:T(8,128)}, f32[672,768]{1,0:T(8,128)}, u32[]{:S(2)}, u32[]{:S(2)}) collective-permute-start(f32[672,768]{1,0:T(8,128)} %fusion.11), channel_id=1, source_target_pairs={{0,4},{4,0},{1,5},{5,1},{2,6},{6,2},{3,7},{7,3},{8,12},{12,8},{9,1... | collective-permute-start | bytes 6193160 | tf_op jit(solution)/shard_map/ppermute | solution.py:34
  303.1 42.4 %collective-permute-start.32 = (f32[160,768]{1,0:T(8,128)}, f32[160,768]{1,0:T(8,128)}, u32[]{:S(2)}, u32[]{:S(2)}) collective-permute-start(f32[160,768]{1,0:T(8,128)} %get-tuple-element.28), channel_id=1, source_target_pairs={{0,16},{8,24},{16,0},{24,8},{1,17},{9,25},{17,1},{25,9},{2,18},{10... | collective-permute-start | bytes 1474568 | tf_op jit(solution)/shard_map/ppermute | solution.py:37
  305.2 43.0 %collective-permute-start.33 = (f32[160,768]{1,0:T(8,128)S(1)}, f32[160,768]{1,0:T(8,128)}, u32[]{:S(2)}, u32[]{:S(2)}) collective-permute-start(f32[160,768]{1,0:T(8,128)S(1)} %get-tuple-element.27), channel_id=1, source_target_pairs={{0,24},{8,0},{16,8},{24,16},{1,25},{9,1},{17,9},{25,17},{2,26},{10... | collective-permute-start | bytes 1474568 | tf_op jit(solution)/shard_map/ppermute | solution.py:37
  311.9 39.0 %collective-permute-start.15 = (f32[384,384]{1,0:T(8,128)}, f32[384,384]{1,0:T(8,128)S(1)}, u32[]{:S(2)}, u32[]{:S(2)}) collective-permute-start(f32[384,384]{1,0:T(8,128)} %slice.142), channel_id=1, source_target_pairs={{0,2},{1,3},{2,0},{3,1},{4,6},{5,7},{6,4},{7,5},{8,10},{9,11},{10,... | collective-permute-start | bytes 1769480 | tf_op jit(solution)/shard_map/ppermute | solution.py:43
  378.5 156.3 %reduce-scatter.6.cloned.1.call-start = ((), (), s32[]{:S(2)}) async-start(), calls=%async_computation.4 | async-start | bytes 3440640 | tf_op jit(solution)/shard_map/reduce_scatter | solution.py:137
  390.4 40.0 %collective-permute-start.28 = (f32[672,384]{1,0:T(8,128)S(1)}, f32[672,384]{1,0:T(8,128)S(1)}, u32[]{:S(2)}, u32[]{:S(2)}) collective-permute-start(f32[672,384]{1,0:T(8,128)S(1)} %slice.147), channel_id=1, source_target_pairs={{0,2},{1,3},{2,0},{3,1},{4,6},{5,7},{6,4},{7,5},{8,10},{9,11},{10,... | collective-permute-start | bytes 3096584 | tf_op jit(solution)/shard_map/ppermute | solution.py:43
  413.8 35.5 %collective-permute-start.41 = (f32[480,768]{1,0:T(8,128)}, f32[480,768]{1,0:T(8,128)}, u32[]{:S(2)}, u32[]{:S(2)}) collective-permute-start(f32[480,768]{1,0:T(8,128)} %fusion.21), channel_id=1, source_target_pairs={{0,4},{4,0},{1,5},{5,1},{2,6},{6,2},{3,7},{7,3},{8,12},{12,8},{9,1... | collective-permute-start | bytes 4423688 | tf_op jit(solution)/shard_map/ppermute | solution.py:34
  432.9 183.1 %reduce-scatter.8.cloned.1.call-start = ((), (), s32[]{:S(2)}) async-start(), calls=%async_computation.5 | async-start | bytes 2457600 | tf_op jit(solution)/shard_map/reduce_scatter | solution.py:137
  433.4 47.7 %collective-permute-start.46 = (f32[512,768]{1,0:T(8,128)}, f32[512,768]{1,0:T(8,128)S(1)}, u32[]{:S(2)}, u32[]{:S(2)}) collective-permute-start(f32[512,768]{1,0:T(8,128)} %fusion.16), channel_id=1, source_target_pairs={{0,4},{4,0},{1,5},{5,1},{2,6},{6,2},{3,7},{7,3},{8,12},{12,8},{9,1... | collective-permute-start | bytes 4718600 | tf_op jit(solution)/shard_map/ppermute | solution.py:34
  439.6 54.0 %collective-permute-start.44 = (f32[480,768]{1,0:T(8,128)}, f32[480,768]{1,0:T(8,128)}, u32[]{:S(2)}, u32[]{:S(2)}) collective-permute-start(f32[480,768]{1,0:T(8,128)} %fusion.47), channel_id=1, source_target_pairs={{0,1},{1,0},{2,3},{3,2},{4,5},{5,4},{6,7},{7,6},{8,9},{9,8},{10,11... | collective-permute-start | bytes 4423688 | tf_op jit(solution)/shard_map/ppermute | solution.py:40
  453.9 44.8 %collective-permute-start.42 = (f32[480,768]{1,0:T(8,128)}, f32[480,768]{1,0:T(8,128)}, u32[]{:S(2)}, u32[]{:S(2)}) collective-permute-start(f32[480,768]{1,0:T(8,128)} %fusion.48), channel_id=1, source_target_pairs={{0,1},{1,0},{2,3},{3,2},{4,5},{5,4},{6,7},{7,6},{8,9},{9,8},{10,11... | collective-permute-start | bytes 4423688 | tf_op jit(solution)/shard_map/ppermute | solution.py:40
  457.2 46.5 %collective-permute-start.49 = (f32[512,768]{1,0:T(8,128)}, f32[512,768]{1,0:T(8,128)}, u32[]{:S(2)}, u32[]{:S(2)}) collective-permute-start(f32[512,768]{1,0:T(8,128)} %fusion.45), channel_id=1, source_target_pairs={{0,1},{1,0},{2,3},{3,2},{4,5},{5,4},{6,7},{7,6},{8,9},{9,8},{10,11... | collective-permute-start | bytes 4718600 | tf_op jit(solution)/shard_map/ppermute | solution.py:40
  508.3 41.4 %collective-permute-start.50 = (f32[512,384]{1,0:T(8,128)}, f32[512,384]{1,0:T(8,128)}, u32[]{:S(2)}, u32[]{:S(2)}) collective-permute-start(f32[512,384]{1,0:T(8,128)} %slice.169), channel_id=1, source_target_pairs={{0,2},{1,3},{2,0},{3,1},{4,6},{5,7},{6,4},{7,5},{8,10},{9,11},{10,... | collective-permute-start | bytes 2359304 | tf_op jit(solution)/shard_map/ppermute | solution.py:43
  513.3 52.6 %collective-permute-start.48 = (f32[512,384]{1,0:T(8,128)S(1)}, f32[512,384]{1,0:T(8,128)S(1)}, u32[]{:S(2)}, u32[]{:S(2)}) collective-permute-start(f32[512,384]{1,0:T(8,128)S(1)} %slice.167), channel_id=1, source_target_pairs={{0,2},{1,3},{2,0},{3,1},{4,6},{5,7},{6,4},{7,5},{8,10},{9,11},{10,... | collective-permute-start | bytes 2359304 | tf_op jit(solution)/shard_map/ppermute | solution.py:43
  (80 other events, 1085.6 us)
Sparse Core Ops, SparseCore 0:
  46.2 37.7 all-gather.6
  96.9 57.6 all-gather.8
  156.7 44.1 all-gather.10
  378.7 32.8 reduce-scatter.3
  433.0 52.1 reduce-scatter.5
  534.9 39.8 reduce-scatter.7
